TPU v7x, 128 devices: a whole 4x4x4 slice. The times are simulated.
128 devices in a mesh: grid: 16 (over z_lo, y, core), sta: 8 (over z_hi, x).
Axes of the slice: x: 4, y: 4, z: 4 (z_hi: 2, z_lo: 2; z = z_hi * 2 + z_lo), core: 2. Of those that a mesh axis runs over, the one named last changes fastest.
Arguments:
- spectra: bfloat16 [64, 2, 6144], P(None, None, 'sta'), may hold values from -6 to 6
- lag_samples: int32 [16, 6144], P('grid', 'sta'), may hold values from 0 to 5999
- slowness: bfloat16 [16, 3, 6144], P('grid', None, 'sta'), may hold values from -3 to 3
- spread_taps: float32 [3, 17], replicated, may hold values from 0.02 to 0.2
Outputs:
- stacked: float32 [16, 32, 8, 128], P('grid')
- deblurred: float32 [16, 32, 8, 128], P('grid')
All inputs are finite; a program needn't handle non-finite values.
Results may differ from a plain program's by a relative error of at most 0.0015.
Values may be sent and summed in bfloat16 or wider, within the bound.
A program may use at most 64 MiB of HBM per device.

v0:
```python
import math
import jax
import jax.numpy as jnp
from jax import lax
from jax.sharding import PartitionSpec as P

STATIONS = 6144
FREQS = 64
F0 = 600
NT = 6000
TAPS = 17
HALF = 8
ITERS = 4
CX = 32
CY = 8
CZ = 128
TWO_PI = 2.0 * math.pi
BACKGROUND = 0.05


def with_halo(array, sides, width):
    for axis, dim in sides:
        size, length = (lax.axis_size(axis), array.shape[dim])
        up = [(i, (i + 1) % size) for i in range(size - 1)]
        down = [(j, i) for i, j in up]
        last = lax.slice_in_dim(array, length - width, length, axis=dim)
        leading = lax.slice_in_dim(array, 0, width, axis=dim)
        before = lax.ppermute(last, axis, up)
        after = lax.ppermute(leading, axis, down)
        array = jnp.concatenate([before, array, after], axis=dim)
    return array


def align_rows(spectra, lag_row):
    bins = F0 + jnp.arange(FREQS, dtype=jnp.int32)
    cycles = bins[:, None] * lag_row[None, :] % NT
    turned = cycles.astype(jnp.float32) * (TWO_PI / NT)
    cosine = jnp.cos(turned)
    sine = jnp.sin(turned)
    real_in = spectra[:, 0, :].astype(jnp.float32)
    imag_in = spectra[:, 1, :].astype(jnp.float32)
    real_out = real_in * cosine + imag_in * sine
    imag_out = imag_in * cosine - real_in * sine
    return jnp.stack([real_out, imag_out], axis=1).astype(jnp.bfloat16)


def beam_freq(freq, aligned_row, slow_rows):
    omega = (F0 + freq).astype(jnp.float32) * (TWO_PI / NT)
    slow = slow_rows.astype(jnp.float32)
    x_coord = jnp.arange(CX, dtype=jnp.float32) - (CX - 1) / 2.0
    y_coord = jnp.arange(CY, dtype=jnp.float32) - (CY - 1) / 2.0
    z_coord = jnp.arange(CZ, dtype=jnp.float32) - (CZ - 1) / 2.0
    phase_x = (omega * slow[0])[None, :] * x_coord[:, None]
    phase_y = (omega * slow[1])[None, :] * y_coord[:, None]
    phase = phase_x[:, None, :] + phase_y[None, :, :]
    cosine = jnp.cos(phase)
    sine = jnp.sin(phase)
    real_in = aligned_row[0].astype(jnp.float32)[None, None, :]
    imag_in = aligned_row[1].astype(jnp.float32)[None, None, :]
    front_real = (real_in * cosine + imag_in * sine).astype(jnp.bfloat16).reshape(CX * CY, -1)
    front_imag = (imag_in * cosine - real_in * sine).astype(jnp.bfloat16).reshape(CX * CY, -1)
    left_side = jnp.concatenate([front_real, front_imag], axis=1)
    phase_z = (omega * slow[2])[:, None] * z_coord[None, :]
    depth_real = jnp.cos(phase_z).astype(jnp.bfloat16)
    depth_imag = jnp.sin(phase_z).astype(jnp.bfloat16)
    upper_rows = jnp.concatenate([depth_real, -depth_imag], axis=1)
    lower_rows = jnp.concatenate([depth_imag, depth_real], axis=1)
    right_side = jnp.concatenate([upper_rows, lower_rows], axis=0)
    return jnp.dot(left_side, right_side, preferred_element_type=jnp.float32)


def freq_beams(freq_ids, aligned_rows, slow_rows):
    return lax.map(lambda pair: beam_freq(pair[0], pair[1], slow_rows), (freq_ids, aligned_rows))


def band_matrix(taps, length):
    rows = jnp.arange(length, dtype=jnp.int32)[:, None]
    columns = jnp.arange(length + 2 * HALF, dtype=jnp.int32)[None, :]
    offset = columns - rows
    picks = jnp.arange(TAPS, dtype=jnp.int32)[:, None, None]
    return jnp.sum(jnp.where(offset[None] == picks, taps[:, None, None], 0.0), axis=0)


def blur(volume, bands):
    band_x, square_y, square_z = bands
    padded = with_halo(volume.astype(jnp.bfloat16), (("grid", 0),), HALF).astype(volume.dtype)
    along_x = jnp.einsum("ip,pyz->iyz", band_x, padded, precision=lax.Precision.HIGHEST)
    along_y = jnp.einsum("jq,xqz->xjz", square_y, along_x, precision=lax.Precision.HIGHEST)
    return jnp.einsum("xyw,kw->xyk", along_y, square_z, precision=lax.Precision.HIGHEST)


def per_device(spectra, lag_samples, slowness, spread_taps):
    groups = lax.axis_size("sta")
    own_count = FREQS // groups
    first_bin = lax.axis_index("sta") * own_count
    aligned = align_rows(spectra, lag_samples[0])
    own_ids = first_bin + jnp.arange(own_count, dtype=jnp.int32)
    rows = lax.dynamic_slice_in_dim(
        lax.all_gather(aligned, "sta", axis=2, tiled=True), first_bin, own_count, 0
    )
    beams = freq_beams(own_ids, rows, lax.all_gather(slowness, "sta", axis=2, tiled=True)[0])
    squares = jnp.sum(beams * beams, axis=0)
    local_power = squares[:, :CZ] + squares[:, CZ:]
    summed = lax.psum(local_power, "sta")
    stacked = (summed / (FREQS * STATIONS) + BACKGROUND).reshape(CX, CY, CZ)
    square_y = band_matrix(spread_taps[1], CY)[:, HALF : HALF + CY]
    square_z = band_matrix(spread_taps[2], CZ)[:, HALF : HALF + CZ]
    bands = (band_matrix(spread_taps[0], CX), square_y, square_z)
    estimate = stacked
    for sweep in range(ITERS):
        blurred = blur(estimate, bands)
        estimate = estimate * blur(stacked / blurred, bands)
    return (stacked[None], estimate[None])


def solution(mesh):
    placed = (P(None, None, "sta"), P("grid", "sta"), P("grid", None, "sta"), P())
    return jax.shard_map(
        per_device,
        mesh=mesh,
        in_specs=placed,
        out_specs=(P("grid", None, None, None), P("grid", None, None, None)),
        check_vma=False,
    )
```

profile of v0, /device:TPU:25, one launch (start us, length us, event | category | flops | bytes accessed | tf_op | source)
XLA Modules:
  0.0 648.4 jit_solution(14156776172203744260)
XLA Ops:
  11.0 29.4 %all_gather.7 = bf16[1,3,6144]{2,1,0:T(4,128)(2,1)S(1)} all-gather(bf16[1,3,768]{2,1,0:T(4,128)(2,1)} %param.8), channel_id=1, replica_groups=mesh['grid'=16,'sta'=8] {'sta'}, dimensions={2}, use_global_device_ids=true | all-gather | bytes 41472 | tf_op jit(solution)/shard_map/all_gather | solution.py:101
  41.5 21.8 %all-gather.2.cloned.1.call-done = bf16[64,2,6144]{2,0,1:T(8,128)(2,1)} async-done(((bf16[64,2,768]{2,0,1:T(8,128)(2,1)}), bf16[64,2,6144]{2,0,1:T(8,128)(2,1)}) %all-gather.2.cloned.1.call-update) | async-done | bytes 1572880 | tf_op jit(solution)/shard_map/all_gather | solution.py:99
  64.4 408.7 %while.12 = (s32[]{:T(128)}, f32[8,256,256]{2,1,0:T(8,128)S(1)}, bf16[8,2,6144]{2,1,0:T(2,128)(2,1)S(1)}, s32[8]{0:T(128)S(1)}, bf16[3,6144]{1,0:T(4,128)(2,1)S(...) while((s32[]{:T(128)}, f32[8,256,256]{2,1,0:T(8,128)S(1)}, ...), condition=%wide.region_1.2_spmd, body=%wide.region_0.1_spmd.sunk | while | flops 1669103744 | bytes 24729580 | solution.py:73
  66.0 23.7 %fusion.136 = (bf16[256,6144]{1,0:T(8,128)(2,1)S(1)}, bf16[256,6144]{1,0:T(8,128)(2,1)S(1)}) fusion(f32[6144]{0:T(1024)S(1)} %bitcast.160, f32[8,6144]{1,0:T(8,128)S(1)} %broadcast_multiply_fusion.4, f32[32,6144]{1,0:T(8,128)S(1)} %broadcast_multiply_fusion.5, f32[6144]{0:T(1024)S(1)} %bitcast.159), kind=kLoop, calls=%fused_computation.6.clone.1 | loop fusion | flops 14155776 | bytes 7323648 | tf_op jit(solution)/shard_map/while/body/eval_jaxpr/convert_element_type | solution.py:60
  89.8 12.3 %fusion.134 = (bf16[6144,128]{1,0:T(8,128)(2,1)S(1)}, bf16[6144,128]{1,0:T(8,128)(2,1)S(1)}) fusion(f32[128]{0:T(128)S(1)} %iota_add_fusion.8, f32[6144]{0:T(1024)S(1)} %bitcast.157), kind=kLoop, calls=%fused_computation.26.clone.2 | loop fusion | flops 2359296 | bytes 3170816 | tf_op jit(solution)/shard_map/while/body/eval_jaxpr/convert_element_type | solution.py:65
  102.1 11.5 %fusion.135 = bf16[6144,128]{1,0:T(8,128)(2,1)S(1)} fusion(f32[128]{0:T(128)S(1)} %iota_add_fusion.8, f32[6144]{0:T(1024)S(1)} %bitcast.158), kind=kLoop, calls=%fused_computation.30.clone.1 | loop fusion | flops 3932160 | bytes 1597952 | tf_op jit(solution)/shard_map/while/body/eval_jaxpr/neg | solution.py:66
  117.1 23.7 %fusion.136 = (bf16[256,6144]{1,0:T(8,128)(2,1)S(1)}, bf16[256,6144]{1,0:T(8,128)(2,1)S(1)}) fusion(f32[6144]{0:T(1024)S(1)} %bitcast.160, f32[8,6144]{1,0:T(8,128)S(1)} %broadcast_multiply_fusion.4, f32[32,6144]{1,0:T(8,128)S(1)} %broadcast_multiply_fusion.5, f32[6144]{0:T(1024)S(1)} %bitcast.159), kind=kLoop, calls=%fused_computation.6.clone.1 | loop fusion | flops 14155776 | bytes 7323648 | tf_op jit(solution)/shard_map/while/body/eval_jaxpr/convert_element_type | solution.py:60
  140.9 12.3 %fusion.134 = (bf16[6144,128]{1,0:T(8,128)(2,1)S(1)}, bf16[6144,128]{1,0:T(8,128)(2,1)S(1)}) fusion(f32[128]{0:T(128)S(1)} %iota_add_fusion.8, f32[6144]{0:T(1024)S(1)} %bitcast.157), kind=kLoop, calls=%fused_computation.26.clone.2 | loop fusion | flops 2359296 | bytes 3170816 | tf_op jit(solution)/shard_map/while/body/eval_jaxpr/convert_element_type | solution.py:65
  153.2 11.5 %fusion.135 = bf16[6144,128]{1,0:T(8,128)(2,1)S(1)} fusion(f32[128]{0:T(128)S(1)} %iota_add_fusion.8, f32[6144]{0:T(1024)S(1)} %bitcast.158), kind=kLoop, calls=%fused_computation.30.clone.1 | loop fusion | flops 3932160 | bytes 1597952 | tf_op jit(solution)/shard_map/while/body/eval_jaxpr/neg | solution.py:66
  168.2 23.7 %fusion.136 = (bf16[256,6144]{1,0:T(8,128)(2,1)S(1)}, bf16[256,6144]{1,0:T(8,128)(2,1)S(1)}) fusion(f32[6144]{0:T(1024)S(1)} %bitcast.160, f32[8,6144]{1,0:T(8,128)S(1)} %broadcast_multiply_fusion.4, f32[32,6144]{1,0:T(8,128)S(1)} %broadcast_multiply_fusion.5, f32[6144]{0:T(1024)S(1)} %bitcast.159), kind=kLoop, calls=%fused_computation.6.clone.1 | loop fusion | flops 14155776 | bytes 7323648 | tf_op jit(solution)/shard_map/while/body/eval_jaxpr/convert_element_type | solution.py:60
  192.0 12.3 %fusion.134 = (bf16[6144,128]{1,0:T(8,128)(2,1)S(1)}, bf16[6144,128]{1,0:T(8,128)(2,1)S(1)}) fusion(f32[128]{0:T(128)S(1)} %iota_add_fusion.8, f32[6144]{0:T(1024)S(1)} %bitcast.157), kind=kLoop, calls=%fused_computation.26.clone.2 | loop fusion | flops 2359296 | bytes 3170816 | tf_op jit(solution)/shard_map/while/body/eval_jaxpr/convert_element_type | solution.py:65
  204.3 11.5 %fusion.135 = bf16[6144,128]{1,0:T(8,128)(2,1)S(1)} fusion(f32[128]{0:T(128)S(1)} %iota_add_fusion.8, f32[6144]{0:T(1024)S(1)} %bitcast.158), kind=kLoop, calls=%fused_computation.30.clone.1 | loop fusion | flops 3932160 | bytes 1597952 | tf_op jit(solution)/shard_map/while/body/eval_jaxpr/neg | solution.py:66
  219.3 23.7 %fusion.136 = (bf16[256,6144]{1,0:T(8,128)(2,1)S(1)}, bf16[256,6144]{1,0:T(8,128)(2,1)S(1)}) fusion(f32[6144]{0:T(1024)S(1)} %bitcast.160, f32[8,6144]{1,0:T(8,128)S(1)} %broadcast_multiply_fusion.4, f32[32,6144]{1,0:T(8,128)S(1)} %broadcast_multiply_fusion.5, f32[6144]{0:T(1024)S(1)} %bitcast.159), kind=kLoop, calls=%fused_computation.6.clone.1 | loop fusion | flops 14155776 | bytes 7323648 | tf_op jit(solution)/shard_map/while/body/eval_jaxpr/convert_element_type | solution.py:60
  243.0 12.3 %fusion.134 = (bf16[6144,128]{1,0:T(8,128)(2,1)S(1)}, bf16[6144,128]{1,0:T(8,128)(2,1)S(1)}) fusion(f32[128]{0:T(128)S(1)} %iota_add_fusion.8, f32[6144]{0:T(1024)S(1)} %bitcast.157), kind=kLoop, calls=%fused_computation.26.clone.2 | loop fusion | flops 2359296 | bytes 3170816 | tf_op jit(solution)/shard_map/while/body/eval_jaxpr/convert_element_type | solution.py:65
  255.4 11.5 %fusion.135 = bf16[6144,128]{1,0:T(8,128)(2,1)S(1)} fusion(f32[128]{0:T(128)S(1)} %iota_add_fusion.8, f32[6144]{0:T(1024)S(1)} %bitcast.158), kind=kLoop, calls=%fused_computation.30.clone.1 | loop fusion | flops 3932160 | bytes 1597952 | tf_op jit(solution)/shard_map/while/body/eval_jaxpr/neg | solution.py:66
  270.4 23.7 %fusion.136 = (bf16[256,6144]{1,0:T(8,128)(2,1)S(1)}, bf16[256,6144]{1,0:T(8,128)(2,1)S(1)}) fusion(f32[6144]{0:T(1024)S(1)} %bitcast.160, f32[8,6144]{1,0:T(8,128)S(1)} %broadcast_multiply_fusion.4, f32[32,6144]{1,0:T(8,128)S(1)} %broadcast_multiply_fusion.5, f32[6144]{0:T(1024)S(1)} %bitcast.159), kind=kLoop, calls=%fused_computation.6.clone.1 | loop fusion | flops 14155776 | bytes 7323648 | tf_op jit(solution)/shard_map/while/body/eval_jaxpr/convert_element_type | solution.py:60
  294.1 12.3 %fusion.134 = (bf16[6144,128]{1,0:T(8,128)(2,1)S(1)}, bf16[6144,128]{1,0:T(8,128)(2,1)S(1)}) fusion(f32[128]{0:T(128)S(1)} %iota_add_fusion.8, f32[6144]{0:T(1024)S(1)} %bitcast.157), kind=kLoop, calls=%fused_computation.26.clone.2 | loop fusion | flops 2359296 | bytes 3170816 | tf_op jit(solution)/shard_map/while/body/eval_jaxpr/convert_element_type | solution.py:65
  306.5 11.5 %fusion.135 = bf16[6144,128]{1,0:T(8,128)(2,1)S(1)} fusion(f32[128]{0:T(128)S(1)} %iota_add_fusion.8, f32[6144]{0:T(1024)S(1)} %bitcast.158), kind=kLoop, calls=%fused_computation.30.clone.1 | loop fusion | flops 3932160 | bytes 1597952 | tf_op jit(solution)/shard_map/while/body/eval_jaxpr/neg | solution.py:66
  321.5 23.7 %fusion.136 = (bf16[256,6144]{1,0:T(8,128)(2,1)S(1)}, bf16[256,6144]{1,0:T(8,128)(2,1)S(1)}) fusion(f32[6144]{0:T(1024)S(1)} %bitcast.160, f32[8,6144]{1,0:T(8,128)S(1)} %broadcast_multiply_fusion.4, f32[32,6144]{1,0:T(8,128)S(1)} %broadcast_multiply_fusion.5, f32[6144]{0:T(1024)S(1)} %bitcast.159), kind=kLoop, calls=%fused_computation.6.clone.1 | loop fusion | flops 14155776 | bytes 7323648 | tf_op jit(solution)/shard_map/while/body/eval_jaxpr/convert_element_type | solution.py:60
  345.2 12.3 %fusion.134 = (bf16[6144,128]{1,0:T(8,128)(2,1)S(1)}, bf16[6144,128]{1,0:T(8,128)(2,1)S(1)}) fusion(f32[128]{0:T(128)S(1)} %iota_add_fusion.8, f32[6144]{0:T(1024)S(1)} %bitcast.157), kind=kLoop, calls=%fused_computation.26.clone.2 | loop fusion | flops 2359296 | bytes 3170816 | tf_op jit(solution)/shard_map/while/body/eval_jaxpr/convert_element_type | solution.py:65
  357.6 11.5 %fusion.135 = bf16[6144,128]{1,0:T(8,128)(2,1)S(1)} fusion(f32[128]{0:T(128)S(1)} %iota_add_fusion.8, f32[6144]{0:T(1024)S(1)} %bitcast.158), kind=kLoop, calls=%fused_computation.30.clone.1 | loop fusion | flops 3932160 | bytes 1597952 | tf_op jit(solution)/shard_map/while/body/eval_jaxpr/neg | solution.py:66
  372.5 23.7 %fusion.136 = (bf16[256,6144]{1,0:T(8,128)(2,1)S(1)}, bf16[256,6144]{1,0:T(8,128)(2,1)S(1)}) fusion(f32[6144]{0:T(1024)S(1)} %bitcast.160, f32[8,6144]{1,0:T(8,128)S(1)} %broadcast_multiply_fusion.4, f32[32,6144]{1,0:T(8,128)S(1)} %broadcast_multiply_fusion.5, f32[6144]{0:T(1024)S(1)} %bitcast.159), kind=kLoop, calls=%fused_computation.6.clone.1 | loop fusion | flops 14155776 | bytes 7323648 | tf_op jit(solution)/shard_map/while/body/eval_jaxpr/convert_element_type | solution.py:60
  396.3 12.3 %fusion.134 = (bf16[6144,128]{1,0:T(8,128)(2,1)S(1)}, bf16[6144,128]{1,0:T(8,128)(2,1)S(1)}) fusion(f32[128]{0:T(128)S(1)} %iota_add_fusion.8, f32[6144]{0:T(1024)S(1)} %bitcast.157), kind=kLoop, calls=%fused_computation.26.clone.2 | loop fusion | flops 2359296 | bytes 3170816 | tf_op jit(solution)/shard_map/while/body/eval_jaxpr/convert_element_type | solution.py:65
  408.6 11.5 %fusion.135 = bf16[6144,128]{1,0:T(8,128)(2,1)S(1)} fusion(f32[128]{0:T(128)S(1)} %iota_add_fusion.8, f32[6144]{0:T(1024)S(1)} %bitcast.158), kind=kLoop, calls=%fused_computation.30.clone.1 | loop fusion | flops 3932160 | bytes 1597952 | tf_op jit(solution)/shard_map/while/body/eval_jaxpr/neg | solution.py:66
  423.6 23.7 %fusion.136 = (bf16[256,6144]{1,0:T(8,128)(2,1)S(1)}, bf16[256,6144]{1,0:T(8,128)(2,1)S(1)}) fusion(f32[6144]{0:T(1024)S(1)} %bitcast.160, f32[8,6144]{1,0:T(8,128)S(1)} %broadcast_multiply_fusion.4, f32[32,6144]{1,0:T(8,128)S(1)} %broadcast_multiply_fusion.5, f32[6144]{0:T(1024)S(1)} %bitcast.159), kind=kLoop, calls=%fused_computation.6.clone.1 | loop fusion | flops 14155776 | bytes 7323648 | tf_op jit(solution)/shard_map/while/body/eval_jaxpr/convert_element_type | solution.py:60
  447.4 12.3 %fusion.134 = (bf16[6144,128]{1,0:T(8,128)(2,1)S(1)}, bf16[6144,128]{1,0:T(8,128)(2,1)S(1)}) fusion(f32[128]{0:T(128)S(1)} %iota_add_fusion.8, f32[6144]{0:T(1024)S(1)} %bitcast.157), kind=kLoop, calls=%fused_computation.26.clone.2 | loop fusion | flops 2359296 | bytes 3170816 | tf_op jit(solution)/shard_map/while/body/eval_jaxpr/convert_element_type | solution.py:65
  459.7 11.5 %fusion.135 = bf16[6144,128]{1,0:T(8,128)(2,1)S(1)} fusion(f32[128]{0:T(128)S(1)} %iota_add_fusion.8, f32[6144]{0:T(1024)S(1)} %bitcast.158), kind=kLoop, calls=%fused_computation.30.clone.1 | loop fusion | flops 3932160 | bytes 1597952 | tf_op jit(solution)/shard_map/while/body/eval_jaxpr/neg | solution.py:66
  474.1 78.1 %all-reduce.2.cloned.1.call-done = f32[256,128]{1,0:T(8,128)} async-done(((f32[256,128]{1,0:T(8,128)}), f32[256,128]{1,0:T(8,128)}) %all-reduce.2.cloned.1.call-update) | async-done | bytes 131088 | tf_op jit(solution)/shard_map/psum | solution.py:104
  553.2 8.2 %collective-permute-start = (bf16[8,8,128]{2,0,1:T(8,128)(2,1)S(1)}, bf16[8,8,128]{2,0,1:T(8,128)(2,1)S(1)}, u32[]{:S(2)}, u32[]{:S(2)}) collective-permute-start(bf16[8,8,128]{2,0,1:T(8,128)(2,1)S(1)} %get-tuple-element.119), channel_id=1, source_target_pairs={{0,8},{8,16},{16,24},{24,32},{32,40},{40,48},{48,56},{56,64},{64,7... | collective-permute-start | bytes 49160 | tf_op jit(solution)/shard_map/ppermute | solution.py:28
  563.5 5.1 collective-permute-done.1
  570.4 1.9 collective-permute-start.2
  572.3 2.4 collective-permute-start.3
  574.7 4.8 collective-permute-done.3
  583.1 2.4 collective-permute-start.5
  585.6 4.8 collective-permute-done.5
  591.2 1.9 collective-permute-start.6
  593.1 2.4 collective-permute-start.7
  595.5 4.8 collective-permute-done.7
  603.1 2.6 collective-permute-start.9
  605.6 4.6 collective-permute-done.9
  613.0 2.4 collective-permute-start.11
  615.4 4.8 collective-permute-done.11
  621.0 1.9 collective-permute-start.12
  623.0 2.4 collective-permute-start.13
  625.4 4.8 collective-permute-done.13
  631.0 1.9 collective-permute-start.14
  632.9 2.4 collective-permute-start.15
  636.0 4.1 collective-permute-done.15
  (158 shorter events, 47.3 us)
Async XLA Ops:
  7.2 56.1 %all-gather.2.cloned.1.call-start = ((), (), s32[]{:S(2)}) async-start(), calls=%async_computation | async-start | bytes 1769472 | tf_op jit(solution)/shard_map/all_gather | solution.py:99
  11.0 541.2 %all-reduce.2.cloned.1.call-start = ((), (), s32[]{:S(2)}) async-start(), calls=%async_computation.1 | async-start | bytes 262144 | tf_op jit(solution)/shard_map/psum | solution.py:104
  552.2 38.7 %copy-start = (f32[256,128]{1,0:T(8,128)S(1)}, f32[256,128]{1,0:T(8,128)}, u32[]{:S(2)}) copy-start(f32[256,128]{1,0:T(8,128)} %all-reduce.2.cloned.1.call-done) | copy-start | bytes 393220
  553.2 10.3 %collective-permute-start = (bf16[8,8,128]{2,0,1:T(8,128)(2,1)S(1)}, bf16[8,8,128]{2,0,1:T(8,128)(2,1)S(1)}, u32[]{:S(2)}, u32[]{:S(2)}) collective-permute-start(bf16[8,8,128]{2,0,1:T(8,128)(2,1)S(1)} %get-tuple-element.119), channel_id=1, source_target_pairs={{0,8},{8,16},{16,24},{24,32},{32,40},{40,48},{48,56},{56,64},{64,7... | collective-permute-start | bytes 49160 | tf_op jit(solution)/shard_map/ppermute | solution.py:28
  561.5 7.2 %collective-permute-start.1 = (bf16[8,8,128]{2,0,1:T(8,128)(2,1)S(1)}, bf16[8,8,128]{2,0,1:T(8,128)(2,1)S(1)}, u32[]{:S(2)}, u32[]{:S(2)}) collective-permute-start(bf16[8,8,128]{2,0,1:T(8,128)(2,1)S(1)} %get-tuple-element.120), channel_id=1, source_target_pairs={{8,0},{16,8},{24,16},{32,24},{40,32},{48,40},{56,48},{64,56},{72,6... | collective-permute-start | bytes 49160 | tf_op jit(solution)/shard_map/ppermute | solution.py:29
  570.4 4.3 collective-permute-start.2
  572.3 7.2 %collective-permute-start.3 = (bf16[8,8,128]{2,1,0:T(8,128)(2,1)S(1)}, bf16[8,8,128]{2,1,0:T(8,128)(2,1)S(1)}, u32[]{:S(2)}, u32[]{:S(2)}) collective-permute-start(bf16[8,8,128]{2,1,0:T(8,128)(2,1)S(1)} %get-tuple-element.118), channel_id=1, source_target_pairs={{8,0},{16,8},{24,16},{32,24},{40,32},{48,40},{56,48},{64,56},{72,6... | collective-permute-start | bytes 49160 | tf_op jit(solution)/shard_map/ppermute | solution.py:29
  581.2 4.3 collective-permute-start.4
  583.1 7.2 %collective-permute-start.5 = (bf16[8,8,128]{2,1,0:T(8,128)(2,1)S(1)}, bf16[8,8,128]{2,1,0:T(8,128)(2,1)S(1)}, u32[]{:S(2)}, u32[]{:S(2)}) collective-permute-start(bf16[8,8,128]{2,1,0:T(8,128)(2,1)S(1)} %get-tuple-element.116), channel_id=1, source_target_pairs={{8,0},{16,8},{24,16},{32,24},{40,32},{48,40},{56,48},{64,56},{72,6... | collective-permute-start | bytes 49160 | tf_op jit(solution)/shard_map/ppermute | solution.py:29
  591.2 4.3 collective-permute-start.6
  593.1 7.2 %collective-permute-start.7 = (bf16[8,8,128]{2,1,0:T(8,128)(2,1)S(1)}, bf16[8,8,128]{2,1,0:T(8,128)(2,1)S(1)}, u32[]{:S(2)}, u32[]{:S(2)}) collective-permute-start(bf16[8,8,128]{2,1,0:T(8,128)(2,1)S(1)} %get-tuple-element.114), channel_id=1, source_target_pairs={{8,0},{16,8},{24,16},{32,24},{40,32},{48,40},{56,48},{64,56},{72,6... | collective-permute-start | bytes 49160 | tf_op jit(solution)/shard_map/ppermute | solution.py:29
  601.1 4.5 collective-permute-start.8
  603.1 7.2 %collective-permute-start.9 = (bf16[8,8,128]{2,1,0:T(8,128)(2,1)S(1)}, bf16[8,8,128]{2,1,0:T(8,128)(2,1)S(1)}, u32[]{:S(2)}, u32[]{:S(2)}) collective-permute-start(bf16[8,8,128]{2,1,0:T(8,128)(2,1)S(1)} %get-tuple-element.112), channel_id=1, source_target_pairs={{8,0},{16,8},{24,16},{32,24},{40,32},{48,40},{56,48},{64,56},{72,6... | collective-permute-start | bytes 49160 | tf_op jit(solution)/shard_map/ppermute | solution.py:29
  611.1 4.3 collective-permute-start.10
  613.0 7.2 %collective-permute-start.11 = (bf16[8,8,128]{2,1,0:T(8,128)(2,1)S(1)}, bf16[8,8,128]{2,1,0:T(8,128)(2,1)S(1)}, u32[]{:S(2)}, u32[]{:S(2)}) collective-permute-start(bf16[8,8,128]{2,1,0:T(8,128)(2,1)S(1)} %get-tuple-element.110), channel_id=1, source_target_pairs={{8,0},{16,8},{24,16},{32,24},{40,32},{48,40},{56,48},{64,56},{72,6... | collective-permute-start | bytes 49160 | tf_op jit(solution)/shard_map/ppermute | solution.py:29
  621.0 4.3 collective-permute-start.12
  623.0 7.2 %collective-permute-start.13 = (bf16[8,8,128]{2,1,0:T(8,128)(2,1)S(1)}, bf16[8,8,128]{2,1,0:T(8,128)(2,1)S(1)}, u32[]{:S(2)}, u32[]{:S(2)}) collective-permute-start(bf16[8,8,128]{2,1,0:T(8,128)(2,1)S(1)} %get-tuple-element.108), channel_id=1, source_target_pairs={{8,0},{16,8},{24,16},{32,24},{40,32},{48,40},{56,48},{64,56},{72,6... | collective-permute-start | bytes 49160 | tf_op jit(solution)/shard_map/ppermute | solution.py:29
  631.0 5.0 collective-permute-start.14
  632.9 7.2 %collective-permute-start.15 = (bf16[8,8,128]{2,1,0:T(8,128)(2,1)S(1)}, bf16[8,8,128]{2,1,0:T(8,128)(2,1)S(1)}, u32[]{:S(2)}, u32[]{:S(2)}) collective-permute-start(bf16[8,8,128]{2,1,0:T(8,128)(2,1)S(1)} %get-tuple-element.106), channel_id=1, source_target_pairs={{8,0},{16,8},{24,16},{32,24},{40,32},{48,40},{56,48},{64,56},{72,6... | collective-permute-start | bytes 49160 | tf_op jit(solution)/shard_map/ppermute | solution.py:29
Sparse Core Ops, SparseCore 0:
  11.1 52.1 all-gather.1
  474.1 78.0 all-reduce.1
where the time goes:
time: 649 us; the launch traced here: 648 us
  other arithmetic  389 us (60%)
  waiting for transfers between devices  138 us (21%)
  starting transfers between devices  40.7 us (6%)
  blocking collectives  29.4 us (5%)
  matrix products  23.3 us (4%)
  between operations  14.6 us (2%)
  local copies, waits for them, and re-layouts  8.06 us (1%)
    convert_element_type x8, other arithmetic, beam_freq(): (real_in * cosine + imag_in * sine).astype(jnp.bfloat16)  190 us
    convert_element_type x8, other arithmetic, beam_freq(): depth_imag = jnp.sin(phase_z).astype(jnp.bfloat16)  98.6 us
    neg x8, other arithmetic, beam_freq(): upper_rows = jnp.concatenate([depth_real, -depth_imag], axis=1)  92.1 us
    psum x1, waiting for transfers between devices, per_device(): summed = lax.psum(local_power, 'sta')  78.1 us
    ppermute x8, waiting for transfers between devices, with_halo(): after = lax.ppermute(leading, axis, down)  37.6 us
    all_gather x1, blocking collectives, per_device(): lax.all_gather(slowness, 'sta', axis=2, tiled=True)[0]  29.4 us
    all_gather x1, waiting for transfers between devices, per_device(): lax.all_gather(aligned, 'sta', axis=2, tiled=True)  21.8 us
    ppermute x8, starting transfers between devices, with_halo(): before = lax.ppermute(last, axis, up)  21.7 us
  transfers between devices with their start and end apart: 18, of which 10 were waited for; matrix products, arithmetic and copies ran while one was open for 0% of the time, Pallas kernels for 0%

commit v1 on v0

--- a/solution.py
+++ b/solution.py
@@ -101,7 +101,7 @@
     beams = freq_beams(own_ids, rows, lax.all_gather(slowness, "sta", axis=2, tiled=True)[0])
     squares = jnp.sum(beams * beams, axis=0)
     local_power = squares[:, :CZ] + squares[:, CZ:]
-    summed = lax.psum(local_power, "sta")
+    summed = jnp.sum(lax.all_gather(local_power, "sta"), axis=0)
     stacked = (summed / (FREQS * STATIONS) + BACKGROUND).reshape(CX, CY, CZ)
     square_y = band_matrix(spread_taps[1], CY)[:, HALF : HALF + CY]
     square_z = band_matrix(spread_taps[2], CZ)[:, HALF : HALF + CZ]

time: 649 us -> 611 us (0.941)
  waiting for transfers between devices: 138 us -> 106 us
    psum x1 -> x0, waiting for transfers between devices: 78.1 us -> none  [per_device(): summed = lax.psum(local_power, 'sta')]
    all_gather x0 -> x1, waiting for transfers between devices: none -> 45.8 us  [per_device(): summed = jnp.sum(lax.all_gather(local_power, 'sta'), axis=0)]
where the time goes in v1:
time: 611 us; the launch traced here: 610 us
  other arithmetic  389 us (64%)
  waiting for transfers between devices  106 us (17%)
  starting transfers between devices  36.1 us (6%)
  blocking collectives  29.4 us (5%)
  matrix products  21.5 us (4%)
  between operations  14.6 us (2%)
  local copies, waits for them, and re-layouts  7.27 us (1%)
    convert_element_type x8, other arithmetic, beam_freq(): (real_in * cosine + imag_in * sine).astype(jnp.bfloat16)  190 us
    convert_element_type x8, other arithmetic, beam_freq(): depth_imag = jnp.sin(phase_z).astype(jnp.bfloat16)  98.6 us
    neg x8, other arithmetic, beam_freq(): upper_rows = jnp.concatenate([depth_real, -depth_imag], axis=1)  92.1 us
    all_gather x1, waiting for transfers between devices, per_device(): summed = jnp.sum(lax.all_gather(local_power, 'sta'), axis=0)  45.8 us
    ppermute x8, waiting for transfers between devices, with_halo(): after = lax.ppermute(leading, axis, down)  37.6 us
    all_gather x1, blocking collectives, per_device(): lax.all_gather(slowness, 'sta', axis=2, tiled=True)[0]  29.4 us
    all_gather x1, waiting for transfers between devices, per_device(): lax.all_gather(aligned, 'sta', axis=2, tiled=True)  22.8 us
    ppermute x8, starting transfers between devices, with_halo(): after = lax.ppermute(leading, axis, down)  18.9 us
  transfers between devices with their start and end apart: 18, of which 10 were waited for; matrix products, arithmetic and copies ran while one was open for 0% of the time, Pallas kernels for 0%

profile of v1, /device:TPU:25, one launch (start us, length us, event | category | flops | bytes accessed | tf_op | source)
XLA Modules:
  0.0 610.3 jit_solution(16295328702318096562)
XLA Ops:
  11.0 29.4 %all_gather.13 = bf16[1,3,6144]{2,1,0:T(4,128)(2,1)S(1)} all-gather(bf16[1,3,768]{2,1,0:T(4,128)(2,1)} %param.8), channel_id=1, replica_groups=mesh['grid'=16,'sta'=8] {'sta'}, dimensions={2}, use_global_device_ids=true | all-gather | bytes 41472 | tf_op jit(solution)/shard_map/all_gather | solution.py:101
  40.5 22.8 %all-gather.4.cloned.1.call-done = bf16[64,2,6144]{2,0,1:T(8,128)(2,1)} async-done(((bf16[64,2,768]{2,0,1:T(8,128)(2,1)}), bf16[64,2,6144]{2,0,1:T(8,128)(2,1)}) %all-gather.4.cloned.1.call-update) | async-done | bytes 1572880 | tf_op jit(solution)/shard_map/all_gather | solution.py:99
  64.4 408.7 %while.12 = (s32[]{:T(128)}, f32[8,256,256]{2,1,0:T(8,128)S(1)}, bf16[8,2,6144]{2,1,0:T(2,128)(2,1)S(1)}, s32[8]{0:T(128)S(1)}, bf16[3,6144]{1,0:T(4,128)(2,1)S(...) while((s32[]{:T(128)}, f32[8,256,256]{2,1,0:T(8,128)S(1)}, ...), condition=%wide.region_1.2_spmd, body=%wide.region_0.1_spmd.sunk | while | flops 1669103744 | bytes 24729580 | solution.py:73
  66.0 23.7 %fusion.136 = (bf16[256,6144]{1,0:T(8,128)(2,1)S(1)}, bf16[256,6144]{1,0:T(8,128)(2,1)S(1)}) fusion(f32[6144]{0:T(1024)S(1)} %bitcast.161, f32[8,6144]{1,0:T(8,128)S(1)} %broadcast_multiply_fusion.4, f32[32,6144]{1,0:T(8,128)S(1)} %broadcast_multiply_fusion.5, f32[6144]{0:T(1024)S(1)} %bitcast.160), kind=kLoop, calls=%fused_computation.6.clone.1 | loop fusion | flops 14155776 | bytes 7323648 | tf_op jit(solution)/shard_map/while/body/eval_jaxpr/convert_element_type | solution.py:60
  89.8 12.3 %fusion.134 = (bf16[6144,128]{1,0:T(8,128)(2,1)S(1)}, bf16[6144,128]{1,0:T(8,128)(2,1)S(1)}) fusion(f32[128]{0:T(128)S(1)} %iota_add_fusion.8, f32[6144]{0:T(1024)S(1)} %bitcast.158), kind=kLoop, calls=%fused_computation.26.clone.2 | loop fusion | flops 2359296 | bytes 3170816 | tf_op jit(solution)/shard_map/while/body/eval_jaxpr/convert_element_type | solution.py:65
  102.1 11.5 %fusion.135 = bf16[6144,128]{1,0:T(8,128)(2,1)S(1)} fusion(f32[128]{0:T(128)S(1)} %iota_add_fusion.8, f32[6144]{0:T(1024)S(1)} %bitcast.159), kind=kLoop, calls=%fused_computation.30.clone.1 | loop fusion | flops 3932160 | bytes 1597952 | tf_op jit(solution)/shard_map/while/body/eval_jaxpr/neg | solution.py:66
  117.1 23.7 %fusion.136 = (bf16[256,6144]{1,0:T(8,128)(2,1)S(1)}, bf16[256,6144]{1,0:T(8,128)(2,1)S(1)}) fusion(f32[6144]{0:T(1024)S(1)} %bitcast.161, f32[8,6144]{1,0:T(8,128)S(1)} %broadcast_multiply_fusion.4, f32[32,6144]{1,0:T(8,128)S(1)} %broadcast_multiply_fusion.5, f32[6144]{0:T(1024)S(1)} %bitcast.160), kind=kLoop, calls=%fused_computation.6.clone.1 | loop fusion | flops 14155776 | bytes 7323648 | tf_op jit(solution)/shard_map/while/body/eval_jaxpr/convert_element_type | solution.py:60
  140.9 12.3 %fusion.134 = (bf16[6144,128]{1,0:T(8,128)(2,1)S(1)}, bf16[6144,128]{1,0:T(8,128)(2,1)S(1)}) fusion(f32[128]{0:T(128)S(1)} %iota_add_fusion.8, f32[6144]{0:T(1024)S(1)} %bitcast.158), kind=kLoop, calls=%fused_computation.26.clone.2 | loop fusion | flops 2359296 | bytes 3170816 | tf_op jit(solution)/shard_map/while/body/eval_jaxpr/convert_element_type | solution.py:65
  153.2 11.5 %fusion.135 = bf16[6144,128]{1,0:T(8,128)(2,1)S(1)} fusion(f32[128]{0:T(128)S(1)} %iota_add_fusion.8, f32[6144]{0:T(1024)S(1)} %bitcast.159), kind=kLoop, calls=%fused_computation.30.clone.1 | loop fusion | flops 3932160 | bytes 1597952 | tf_op jit(solution)/shard_map/while/body/eval_jaxpr/neg | solution.py:66
  168.2 23.7 %fusion.136 = (bf16[256,6144]{1,0:T(8,128)(2,1)S(1)}, bf16[256,6144]{1,0:T(8,128)(2,1)S(1)}) fusion(f32[6144]{0:T(1024)S(1)} %bitcast.161, f32[8,6144]{1,0:T(8,128)S(1)} %broadcast_multiply_fusion.4, f32[32,6144]{1,0:T(8,128)S(1)} %broadcast_multiply_fusion.5, f32[6144]{0:T(1024)S(1)} %bitcast.160), kind=kLoop, calls=%fused_computation.6.clone.1 | loop fusion | flops 14155776 | bytes 7323648 | tf_op jit(solution)/shard_map/while/body/eval_jaxpr/convert_element_type | solution.py:60
  192.0 12.3 %fusion.134 = (bf16[6144,128]{1,0:T(8,128)(2,1)S(1)}, bf16[6144,128]{1,0:T(8,128)(2,1)S(1)}) fusion(f32[128]{0:T(128)S(1)} %iota_add_fusion.8, f32[6144]{0:T(1024)S(1)} %bitcast.158), kind=kLoop, calls=%fused_computation.26.clone.2 | loop fusion | flops 2359296 | bytes 3170816 | tf_op jit(solution)/shard_map/while/body/eval_jaxpr/convert_element_type | solution.py:65
  204.3 11.5 %fusion.135 = bf16[6144,128]{1,0:T(8,128)(2,1)S(1)} fusion(f32[128]{0:T(128)S(1)} %iota_add_fusion.8, f32[6144]{0:T(1024)S(1)} %bitcast.159), kind=kLoop, calls=%fused_computation.30.clone.1 | loop fusion | flops 3932160 | bytes 1597952 | tf_op jit(solution)/shard_map/while/body/eval_jaxpr/neg | solution.py:66
  219.3 23.7 %fusion.136 = (bf16[256,6144]{1,0:T(8,128)(2,1)S(1)}, bf16[256,6144]{1,0:T(8,128)(2,1)S(1)}) fusion(f32[6144]{0:T(1024)S(1)} %bitcast.161, f32[8,6144]{1,0:T(8,128)S(1)} %broadcast_multiply_fusion.4, f32[32,6144]{1,0:T(8,128)S(1)} %broadcast_multiply_fusion.5, f32[6144]{0:T(1024)S(1)} %bitcast.160), kind=kLoop, calls=%fused_computation.6.clone.1 | loop fusion | flops 14155776 | bytes 7323648 | tf_op jit(solution)/shard_map/while/body/eval_jaxpr/convert_element_type | solution.py:60
  243.1 12.3 %fusion.134 = (bf16[6144,128]{1,0:T(8,128)(2,1)S(1)}, bf16[6144,128]{1,0:T(8,128)(2,1)S(1)}) fusion(f32[128]{0:T(128)S(1)} %iota_add_fusion.8, f32[6144]{0:T(1024)S(1)} %bitcast.158), kind=kLoop, calls=%fused_computation.26.clone.2 | loop fusion | flops 2359296 | bytes 3170816 | tf_op jit(solution)/shard_map/while/body/eval_jaxpr/convert_element_type | solution.py:65
  255.4 11.5 %fusion.135 = bf16[6144,128]{1,0:T(8,128)(2,1)S(1)} fusion(f32[128]{0:T(128)S(1)} %iota_add_fusion.8, f32[6144]{0:T(1024)S(1)} %bitcast.159), kind=kLoop, calls=%fused_computation.30.clone.1 | loop fusion | flops 3932160 | bytes 1597952 | tf_op jit(solution)/shard_map/while/body/eval_jaxpr/neg | solution.py:66
  270.4 23.7 %fusion.136 = (bf16[256,6144]{1,0:T(8,128)(2,1)S(1)}, bf16[256,6144]{1,0:T(8,128)(2,1)S(1)}) fusion(f32[6144]{0:T(1024)S(1)} %bitcast.161, f32[8,6144]{1,0:T(8,128)S(1)} %broadcast_multiply_fusion.4, f32[32,6144]{1,0:T(8,128)S(1)} %broadcast_multiply_fusion.5, f32[6144]{0:T(1024)S(1)} %bitcast.160), kind=kLoop, calls=%fused_computation.6.clone.1 | loop fusion | flops 14155776 | bytes 7323648 | tf_op jit(solution)/shard_map/while/body/eval_jaxpr/convert_element_type | solution.py:60
  294.2 12.3 %fusion.134 = (bf16[6144,128]{1,0:T(8,128)(2,1)S(1)}, bf16[6144,128]{1,0:T(8,128)(2,1)S(1)}) fusion(f32[128]{0:T(128)S(1)} %iota_add_fusion.8, f32[6144]{0:T(1024)S(1)} %bitcast.158), kind=kLoop, calls=%fused_computation.26.clone.2 | loop fusion | flops 2359296 | bytes 3170816 | tf_op jit(solution)/shard_map/while/body/eval_jaxpr/convert_element_type | solution.py:65
  306.5 11.5 %fusion.135 = bf16[6144,128]{1,0:T(8,128)(2,1)S(1)} fusion(f32[128]{0:T(128)S(1)} %iota_add_fusion.8, f32[6144]{0:T(1024)S(1)} %bitcast.159), kind=kLoop, calls=%fused_computation.30.clone.1 | loop fusion | flops 3932160 | bytes 1597952 | tf_op jit(solution)/shard_map/while/body/eval_jaxpr/neg | solution.py:66
  321.5 23.7 %fusion.136 = (bf16[256,6144]{1,0:T(8,128)(2,1)S(1)}, bf16[256,6144]{1,0:T(8,128)(2,1)S(1)}) fusion(f32[6144]{0:T(1024)S(1)} %bitcast.161, f32[8,6144]{1,0:T(8,128)S(1)} %broadcast_multiply_fusion.4, f32[32,6144]{1,0:T(8,128)S(1)} %broadcast_multiply_fusion.5, f32[6144]{0:T(1024)S(1)} %bitcast.160), kind=kLoop, calls=%fused_computation.6.clone.1 | loop fusion | flops 14155776 | bytes 7323648 | tf_op jit(solution)/shard_map/while/body/eval_jaxpr/convert_element_type | solution.py:60
  345.2 12.3 %fusion.134 = (bf16[6144,128]{1,0:T(8,128)(2,1)S(1)}, bf16[6144,128]{1,0:T(8,128)(2,1)S(1)}) fusion(f32[128]{0:T(128)S(1)} %iota_add_fusion.8, f32[6144]{0:T(1024)S(1)} %bitcast.158), kind=kLoop, calls=%fused_computation.26.clone.2 | loop fusion | flops 2359296 | bytes 3170816 | tf_op jit(solution)/shard_map/while/body/eval_jaxpr/convert_element_type | solution.py:65
  357.6 11.5 %fusion.135 = bf16[6144,128]{1,0:T(8,128)(2,1)S(1)} fusion(f32[128]{0:T(128)S(1)} %iota_add_fusion.8, f32[6144]{0:T(1024)S(1)} %bitcast.159), kind=kLoop, calls=%fused_computation.30.clone.1 | loop fusion | flops 3932160 | bytes 1597952 | tf_op jit(solution)/shard_map/while/body/eval_jaxpr/neg | solution.py:66
  372.6 23.7 %fusion.136 = (bf16[256,6144]{1,0:T(8,128)(2,1)S(1)}, bf16[256,6144]{1,0:T(8,128)(2,1)S(1)}) fusion(f32[6144]{0:T(1024)S(1)} %bitcast.161, f32[8,6144]{1,0:T(8,128)S(1)} %broadcast_multiply_fusion.4, f32[32,6144]{1,0:T(8,128)S(1)} %broadcast_multiply_fusion.5, f32[6144]{0:T(1024)S(1)} %bitcast.160), kind=kLoop, calls=%fused_computation.6.clone.1 | loop fusion | flops 14155776 | bytes 7323648 | tf_op jit(solution)/shard_map/while/body/eval_jaxpr/convert_element_type | solution.py:60
  396.3 12.3 %fusion.134 = (bf16[6144,128]{1,0:T(8,128)(2,1)S(1)}, bf16[6144,128]{1,0:T(8,128)(2,1)S(1)}) fusion(f32[128]{0:T(128)S(1)} %iota_add_fusion.8, f32[6144]{0:T(1024)S(1)} %bitcast.158), kind=kLoop, calls=%fused_computation.26.clone.2 | loop fusion | flops 2359296 | bytes 3170816 | tf_op jit(solution)/shard_map/while/body/eval_jaxpr/convert_element_type | solution.py:65
  408.7 11.5 %fusion.135 = bf16[6144,128]{1,0:T(8,128)(2,1)S(1)} fusion(f32[128]{0:T(128)S(1)} %iota_add_fusion.8, f32[6144]{0:T(1024)S(1)} %bitcast.159), kind=kLoop, calls=%fused_computation.30.clone.1 | loop fusion | flops 3932160 | bytes 1597952 | tf_op jit(solution)/shard_map/while/body/eval_jaxpr/neg | solution.py:66
  423.6 23.7 %fusion.136 = (bf16[256,6144]{1,0:T(8,128)(2,1)S(1)}, bf16[256,6144]{1,0:T(8,128)(2,1)S(1)}) fusion(f32[6144]{0:T(1024)S(1)} %bitcast.161, f32[8,6144]{1,0:T(8,128)S(1)} %broadcast_multiply_fusion.4, f32[32,6144]{1,0:T(8,128)S(1)} %broadcast_multiply_fusion.5, f32[6144]{0:T(1024)S(1)} %bitcast.160), kind=kLoop, calls=%fused_computation.6.clone.1 | loop fusion | flops 14155776 | bytes 7323648 | tf_op jit(solution)/shard_map/while/body/eval_jaxpr/convert_element_type | solution.py:60
  447.4 12.3 %fusion.134 = (bf16[6144,128]{1,0:T(8,128)(2,1)S(1)}, bf16[6144,128]{1,0:T(8,128)(2,1)S(1)}) fusion(f32[128]{0:T(128)S(1)} %iota_add_fusion.8, f32[6144]{0:T(1024)S(1)} %bitcast.158), kind=kLoop, calls=%fused_computation.26.clone.2 | loop fusion | flops 2359296 | bytes 3170816 | tf_op jit(solution)/shard_map/while/body/eval_jaxpr/convert_element_type | solution.py:65
  459.7 11.5 %fusion.135 = bf16[6144,128]{1,0:T(8,128)(2,1)S(1)} fusion(f32[128]{0:T(128)S(1)} %iota_add_fusion.8, f32[6144]{0:T(1024)S(1)} %bitcast.159), kind=kLoop, calls=%fused_computation.30.clone.1 | loop fusion | flops 3932160 | bytes 1597952 | tf_op jit(solution)/shard_map/while/body/eval_jaxpr/neg | solution.py:66
  474.3 45.8 %all-gather.6.cloned.1.call-done = f32[2048,128]{1,0:T(8,128)} async-done(((f32[256,128]{1,0:T(8,128)}), f32[2048,128]{1,0:T(8,128)}) %all-gather.6.cloned.1.call-update) | async-done | bytes 1048592 | tf_op jit(solution)/shard_map/all_gather | solution.py:104
  521.5 3.7 collective-permute-start
  527.2 5.1 collective-permute-done.1
  533.2 1.9 collective-permute-start.2
  535.1 2.4 collective-permute-start.3
  537.5 4.8 collective-permute-done.3
  545.1 2.4 collective-permute-start.5
  547.5 4.8 collective-permute-done.5
  553.1 1.9 collective-permute-start.6
  555.0 2.4 collective-permute-start.7
  557.4 4.8 collective-permute-done.7
  565.0 2.6 collective-permute-start.9
  567.6 4.6 collective-permute-done.9
  573.0 1.9 collective-permute-start.10
  574.9 2.4 collective-permute-start.11
  577.3 4.8 collective-permute-done.11
  584.9 2.4 collective-permute-start.13
  587.3 4.8 collective-permute-done.13
  592.9 1.9 collective-permute-start.14
  594.8 2.4 collective-permute-start.15
  597.9 4.1 collective-permute-done.15
  (159 shorter events, 45.1 us)
Async XLA Ops:
  7.2 56.1 %all-gather.4.cloned.1.call-start = ((), (), s32[]{:S(2)}) async-start(), calls=%async_computation | async-start | bytes 1769472 | tf_op jit(solution)/shard_map/all_gather | solution.py:99
  11.0 509.2 %all-gather.6.cloned.1.call-start = ((), (), s32[]{:S(2)}) async-start(), calls=%async_computation.1 | async-start | bytes 1179648 | tf_op jit(solution)/shard_map/all_gather | solution.py:104
  64.4 409.6 %copy-start = (f32[3,17]{1,0:T(4,128)S(1)}, f32[3,17]{1,0:T(4,128)}, u32[]{:S(2)}) copy-start(f32[3,17]{1,0:T(4,128)} %param.9) | copy-start | bytes 616
  521.5 5.7 collective-permute-start
  525.2 7.2 %collective-permute-start.1 = (bf16[8,8,128]{2,0,1:T(8,128)(2,1)S(1)}, bf16[8,8,128]{2,0,1:T(8,128)(2,1)S(1)}, u32[]{:S(2)}, u32[]{:S(2)}) collective-permute-start(bf16[8,8,128]{2,0,1:T(8,128)(2,1)S(1)} %get-tuple-element.120), channel_id=1, source_target_pairs={{8,0},{16,8},{24,16},{32,24},{40,32},{48,40},{56,48},{64,56},{72,6... | collective-permute-start | bytes 49160 | tf_op jit(solution)/shard_map/ppermute | solution.py:29
  533.2 4.3 collective-permute-start.2
  535.1 7.2 %collective-permute-start.3 = (bf16[8,8,128]{2,1,0:T(8,128)(2,1)S(1)}, bf16[8,8,128]{2,1,0:T(8,128)(2,1)S(1)}, u32[]{:S(2)}, u32[]{:S(2)}) collective-permute-start(bf16[8,8,128]{2,1,0:T(8,128)(2,1)S(1)} %get-tuple-element.118), channel_id=1, source_target_pairs={{8,0},{16,8},{24,16},{32,24},{40,32},{48,40},{56,48},{64,56},{72,6... | collective-permute-start | bytes 49160 | tf_op jit(solution)/shard_map/ppermute | solution.py:29
  543.1 4.3 collective-permute-start.4
  545.1 7.2 %collective-permute-start.5 = (bf16[8,8,128]{2,1,0:T(8,128)(2,1)S(1)}, bf16[8,8,128]{2,1,0:T(8,128)(2,1)S(1)}, u32[]{:S(2)}, u32[]{:S(2)}) collective-permute-start(bf16[8,8,128]{2,1,0:T(8,128)(2,1)S(1)} %get-tuple-element.116), channel_id=1, source_target_pairs={{8,0},{16,8},{24,16},{32,24},{40,32},{48,40},{56,48},{64,56},{72,6... | collective-permute-start | bytes 49160 | tf_op jit(solution)/shard_map/ppermute | solution.py:29
  553.1 4.3 collective-permute-start.6
  555.0 7.2 %collective-permute-start.7 = (bf16[8,8,128]{2,1,0:T(8,128)(2,1)S(1)}, bf16[8,8,128]{2,1,0:T(8,128)(2,1)S(1)}, u32[]{:S(2)}, u32[]{:S(2)}) collective-permute-start(bf16[8,8,128]{2,1,0:T(8,128)(2,1)S(1)} %get-tuple-element.114), channel_id=1, source_target_pairs={{8,0},{16,8},{24,16},{32,24},{40,32},{48,40},{56,48},{64,56},{72,6... | collective-permute-start | bytes 49160 | tf_op jit(solution)/shard_map/ppermute | solution.py:29
  563.0 4.5 collective-permute-start.8
  565.0 7.2 %collective-permute-start.9 = (bf16[8,8,128]{2,1,0:T(8,128)(2,1)S(1)}, bf16[8,8,128]{2,1,0:T(8,128)(2,1)S(1)}, u32[]{:S(2)}, u32[]{:S(2)}) collective-permute-start(bf16[8,8,128]{2,1,0:T(8,128)(2,1)S(1)} %get-tuple-element.112), channel_id=1, source_target_pairs={{8,0},{16,8},{24,16},{32,24},{40,32},{48,40},{56,48},{64,56},{72,6... | collective-permute-start | bytes 49160 | tf_op jit(solution)/shard_map/ppermute | solution.py:29
  573.0 4.3 collective-permute-start.10
  574.9 7.2 %collective-permute-start.11 = (bf16[8,8,128]{2,1,0:T(8,128)(2,1)S(1)}, bf16[8,8,128]{2,1,0:T(8,128)(2,1)S(1)}, u32[]{:S(2)}, u32[]{:S(2)}) collective-permute-start(bf16[8,8,128]{2,1,0:T(8,128)(2,1)S(1)} %get-tuple-element.110), channel_id=1, source_target_pairs={{8,0},{16,8},{24,16},{32,24},{40,32},{48,40},{56,48},{64,56},{72,6... | collective-permute-start | bytes 49160 | tf_op jit(solution)/shard_map/ppermute | solution.py:29
  582.9 4.3 collective-permute-start.12
  584.9 7.2 %collective-permute-start.13 = (bf16[8,8,128]{2,1,0:T(8,128)(2,1)S(1)}, bf16[8,8,128]{2,1,0:T(8,128)(2,1)S(1)}, u32[]{:S(2)}, u32[]{:S(2)}) collective-permute-start(bf16[8,8,128]{2,1,0:T(8,128)(2,1)S(1)} %get-tuple-element.108), channel_id=1, source_target_pairs={{8,0},{16,8},{24,16},{32,24},{40,32},{48,40},{56,48},{64,56},{72,6... | collective-permute-start | bytes 49160 | tf_op jit(solution)/shard_map/ppermute | solution.py:29
  592.9 5.0 collective-permute-start.14
  594.8 7.2 %collective-permute-start.15 = (bf16[8,8,128]{2,1,0:T(8,128)(2,1)S(1)}, bf16[8,8,128]{2,1,0:T(8,128)(2,1)S(1)}, u32[]{:S(2)}, u32[]{:S(2)}) collective-permute-start(bf16[8,8,128]{2,1,0:T(8,128)(2,1)S(1)} %get-tuple-element.106), channel_id=1, source_target_pairs={{8,0},{16,8},{24,16},{32,24},{40,32},{48,40},{56,48},{64,56},{72,6... | collective-permute-start | bytes 49160 | tf_op jit(solution)/shard_map/ppermute | solution.py:29
Sparse Core Ops, SparseCore 0:
  11.1 52.1 all-gather.3
  474.1 46.0 all-gather.5
